TPU v7x, 32 devices: a whole 2x2x4 slice. The times are simulated.
32 devices in a mesh: row: 4 (over x, core), col: 8 (over z, y).
Axes of the slice: x: 2, y: 2, z: 4, core: 2. Of those that a mesh axis runs over, the one named last changes fastest.
Arguments:
- features: bfloat16 [4096, 256], P(('row', 'col')), may hold values from -192 to 192
- grad_out: bfloat16 [4096, 256], P(('row', 'col')), may hold values from -192 to 192
- tile_weight: bfloat16 [2048, 128, 128], P(('row', 'col')), may hold values from 0 to 256, as said below
- tile_list: int32 [128, 3, 32], P(('row', 'col')), may hold values from -1 to 63, as said below
Outputs:
- aggregated: bfloat16 [4096, 256], P(('row', 'col'))
- feature_grad: bfloat16 [4096, 256], P(('row', 'col'))
Inputs may be any that keep to these rules, and one draw needn't show every extreme that they name: `tile_list`: each column of a list is a slot (tile number, source block below 1, destination block below 8); tile number -1 marks an empty slot, whose blocks are 0. The tile numbers listed by one device are distinct and are 0 to n - 1 for some n between 40 and 64; some device lists all 64. On every device some step has all 32 slots used. Stored tiles that no slot lists take no part. `tile_weight`: entries are whole numbers.
All inputs are finite; a program needn't handle non-finite values.
Results may differ from a plain program's by a relative error of at most 0.017.
Values may be sent and summed in bfloat16 or wider, within the bound.
No kernel may reach another device: no remote copies, remote signals or barrier semaphores. Data moves between devices by JAX's collectives and lax.ppermute only.
A program may use at most 64 MiB of HBM per device.

v0:
```python
import math
import jax
import jax.numpy as jnp
from jax import lax
from jax.sharding import PartitionSpec as P


def passed_along(value, axis, steps):
    count = lax.axis_size(axis)
    pairs = [(source, (source + steps) % count) for source in range(count)]
    return lax.ppermute(value, axis, pairs)


def local(features, grad_out, tile_weight, tile_list):
    step_count = lax.axis_size("row")
    columns = lax.axis_size("col")
    row_pos = lax.axis_index("row")
    slot_count = tile_list.shape[2]
    tiles_here = tile_weight.shape[0]
    tile_len = tile_weight.shape[1]
    feat_width = features.shape[1]
    src_blocks = features.shape[0] // tile_len
    dst_blocks = columns * (grad_out.shape[0] // tile_len)
    flat_ids = tile_list[:, 0, :].reshape(-1)
    flat_step = jnp.arange(step_count * slot_count, dtype=jnp.int32) // slot_count
    matches = (flat_ids[None, :] == jnp.arange(tiles_here, dtype=jnp.int32)[:, None]).astype(
        jnp.int32
    )
    tile_used = jnp.sum(matches, axis=1)
    tile_step = jnp.sum(matches * flat_step[None, :], axis=1)
    tile_src = jnp.sum(matches * tile_list[:, 1, :].reshape(-1)[None, :], axis=1)
    tile_dst = jnp.sum(matches * tile_list[:, 2, :].reshape(-1)[None, :], axis=1)
    owner_row = (row_pos - tile_step) % step_count
    src_slot = owner_row * src_blocks + tile_src
    used_float = tile_used.astype(jnp.float32)
    row_sums = jnp.sum(tile_weight, axis=2, dtype=jnp.float32)
    col_sums = jnp.sum(tile_weight, axis=1, dtype=jnp.float32)
    dst_pick = (tile_dst[:, None] == jnp.arange(dst_blocks, dtype=jnp.int32)[None, :]).astype(
        jnp.float32
    ) * used_float[:, None]
    src_pick = (
        src_slot[:, None] == jnp.arange(step_count * src_blocks, dtype=jnp.int32)[None, :]
    ).astype(jnp.float32) * used_float[:, None]
    dst_terms = jnp.dot(dst_pick.T, row_sums, precision=lax.Precision.HIGHEST).reshape(-1)
    src_terms = jnp.dot(src_pick.T, col_sums, precision=lax.Precision.HIGHEST).reshape(-1)
    src_scale = lax.rsqrt(1.0 + lax.psum_scatter(src_terms, "row", scatter_dimension=0, tiled=True))
    dst_scale = lax.rsqrt(1.0 + lax.psum_scatter(dst_terms, "col", scatter_dimension=0, tiled=True))
    scaled = (features.astype(jnp.float32) * src_scale[:, None]).astype(jnp.bfloat16)
    scaled = scaled.reshape(src_blocks, tile_len, feat_width)
    scaled_grads = (grad_out.astype(jnp.float32) * dst_scale[:, None]).astype(jnp.bfloat16)
    grad_rows = lax.all_gather(scaled_grads, "col", axis=0, tiled=True).reshape(
        dst_blocks, tile_len, feat_width
    )

    def pick_tiles(list_step):
        tile_ids = tile_list[list_step, 0]
        keep_mask = (tile_ids >= 0).astype(jnp.bfloat16)
        chosen = tile_weight[jnp.maximum(tile_ids, 0)] * keep_mask[:, None, None]
        return (chosen, tile_list[list_step, 1], tile_list[list_step, 2])

    def backward_add(accum_total, rows, list_step):
        chosen, src_index, dst_index = pick_tiles(list_step)
        products = jnp.einsum(
            "kij,kif->kjf", chosen, rows[dst_index], preferred_element_type=jnp.float32
        )
        return accum_total.at[src_index].add(products)

    def grad_step(grad_state, step_pos):
        return backward_add(grad_state, grad_rows, step_count - 1 - step_pos)

    def grad_move(grad_state):
        return passed_along(grad_state.astype(jnp.bfloat16), "row", -1).astype(grad_state.dtype)

    partial_zero = jnp.zeros((dst_blocks, tile_len, feat_width), jnp.float32)
    everything = lax.all_gather(scaled, "row", axis=0, tiled=True)
    batch_size = math.gcd(tiles_here, 16)

    def tile_batch(loop_index, partial_value):
        first_tile = loop_index * batch_size
        tile_block = lax.dynamic_slice_in_dim(tile_weight, first_tile, batch_size, 0)
        keep_mask = lax.dynamic_slice_in_dim(tile_used, first_tile, batch_size, 0).astype(
            jnp.bfloat16
        )
        src_index = lax.dynamic_slice_in_dim(src_slot, first_tile, batch_size, 0)
        dst_index = lax.dynamic_slice_in_dim(tile_dst, first_tile, batch_size, 0)
        chosen = tile_block * keep_mask[:, None, None]
        products = jnp.einsum(
            "kij,kjf->kif", chosen, everything[src_index], preferred_element_type=jnp.float32
        )
        return partial_value.at[dst_index].add(products)

    partial_value = lax.fori_loop(0, tiles_here // batch_size, tile_batch, partial_zero)

    def grad_loop(step_pos, grad_state):
        return grad_move(grad_step(grad_state, step_pos))

    grad_state = lax.fori_loop(
        0, step_count - 1, grad_loop, jnp.zeros((src_blocks, tile_len, feat_width), jnp.float32)
    )
    grad_state = grad_step(grad_state, step_count - 1)
    summed = lax.psum_scatter(
        partial_value.reshape(dst_blocks * tile_len, feat_width).astype(jnp.bfloat16),
        "col",
        scatter_dimension=0,
        tiled=True,
    ).astype(jnp.float32)
    aggregated = (summed * dst_scale[:, None]).astype(jnp.bfloat16)
    grads = grad_state.reshape(src_blocks * tile_len, feat_width)
    feature_grad = (grads * src_scale[:, None]).astype(jnp.bfloat16)
    return (aggregated, feature_grad)


def solution(mesh):
    return jax.shard_map(
        local,
        mesh=mesh,
        in_specs=(
            P(("row", "col"), None),
            P(("row", "col"), None),
            P(("row", "col"), None, None),
            P(("row", "col"), None, None),
        ),
        out_specs=(P(("row", "col"), None), P(("row", "col"), None)),
        check_vma=False,
    )
```

profile of v0, /device:TPU:0, one launch (start us, length us, event | category | flops | bytes accessed | tf_op | source)
XLA Modules:
  0.0 244.0 jit_solution(11328118093270040016)
XLA Ops:
  7.2 0.8 fusion.26
  8.1 0.7 fusion.27
  8.8 0.7 fusion.29
  10.1 0.7 fusion.34
  10.8 0.7 copy.13
  11.5 1.3 dynamic-slice.2
  12.9 1.2 dynamic-slice
  15.8 2.3 convert_reduce_fusion
  18.3 8.4 %all-reduce = f32[512]{0:T(512)S(1)} all-reduce(f32[512]{0:T(512)S(1)} %convolution_bitcast_fusion.1), channel_id=3, replica_groups=mesh['row'=4,'col'=8] {'row'}, use_global_device_ids=true, to_apply=%region_5.6.clone | all-reduce | flops 512 | bytes 4096
  26.9 21.7 %all-reduce.1 = f32[1024]{0:T(1024)S(1)} all-reduce(f32[1024]{0:T(1024)S(1)} %convolution_bitcast_fusion), channel_id=5, replica_groups=mesh['row'=4,'col'=8] {'col'}, use_global_device_ids=true, to_apply=%region_11.12.clone | all-reduce | flops 1024 | bytes 8192
  48.8 31.5 %all_gather.7 = bf16[1024,256]{1,0:T(8,128)(2,1)S(1)} all-gather(bf16[128,256]{1,0:T(8,128)(2,1)S(1)} %multiply_convert_fusion), channel_id=1, replica_groups=mesh['row'=4,'col'=8] {'col'}, dimensions={0}, use_global_device_ids=true | all-gather | bytes 589824 | tf_op jit(solution)/shard_map/all_gather | solution.py:51
  80.3 1.7 gather_fusion.3
  82.1 2.0 gather_fusion.4
  84.1 5.0 %fusion.13 = f32[32,128,256]{2,1,0:T(8,128)} fusion(bf16[32,128,256]{2,1,0:T(8,128)(2,1)} %gather_fusion.4, bf16[32,128,128]{2,1,0:T(8,128)(2,1)} %gather_fusion.3, bf16[32]{0:T(256)(128)(2,1)S(1)} %fusion.26), kind=kOutput, calls=%fused_computation.41 | convolution fusion | flops 268959744 | bytes 7340096 | tf_op jit(solution)/shard_map/kij,kif->kjf/dot_general | solution.py:63
  89.0 49.5 %while.30 = (s32[]{:T(128)}, f32[1,128,256]{2,1,0:T(8,128)S(1)}, s32[4,3,32]{2,1,0:T(4,128)S(1)}, bf16[64,128,128]{2,1,0:T(8,128)(2,1)S(1)}, bf16[8,128,256]{2,1...) while((s32[]{:T(128)}, f32[1,128,256]{2,1,0:T(8,128)S(1)}, ...), condition=%wide.region_14.15_spmd.clone, body=%wide.region_12.14_spmd.clone.sunk | while | flops 270109056 | bytes 35530608 | solution.py:97
  89.1 1.7 gather_fusion.2
  91.6 4.3 %fusion.57 = f32[32,128,256]{2,1,0:T(8,128)} fusion(bf16[32,128,256]{2,1,0:T(8,128)(2,1)S(1)} %gather_fusion.1, bf16[32,128,128]{2,1,0:T(8,128)(2,1)} %gather_fusion.2, bf16[32]{0:T(256)(128)(2,1)S(1)} %fusion.56), kind=kOutput, calls=%fused_computation.17.clone.1 | convolution fusion | flops 268959744 | bytes 7340096 | tf_op jit(solution)/shard_map/while/body/eval_jaxpr/kij,kif->kjf/dot_general | solution.py:63
  95.9 6.4 %scatter_fusion.1 = f32[128,256,1]{1,0,2:T(8,128)S(1)} fusion(f32[128,256,1]{1,0,2:T(8,128)S(1)} %select_bitcast_fusion.2, s32[32]{0:T(128)S(1)} %fusion.54, f32[32,128,256]{2,1,0:T(8,128)} %fusion.57), kind=kCustom, calls=%fused_computation.6.clone.clone.1 | custom fusion | flops 1048576 | bytes 12583040 | tf_op jit(solution)/shard_map/while/body/eval_jaxpr/scatter-add | solution.py:66
  102.4 1.9 collective-permute-done
  104.5 1.7 gather_fusion.2
  106.9 4.3 %fusion.57 = f32[32,128,256]{2,1,0:T(8,128)} fusion(bf16[32,128,256]{2,1,0:T(8,128)(2,1)S(1)} %gather_fusion.1, bf16[32,128,128]{2,1,0:T(8,128)(2,1)} %gather_fusion.2, bf16[32]{0:T(256)(128)(2,1)S(1)} %fusion.56), kind=kOutput, calls=%fused_computation.17.clone.1 | convolution fusion | flops 268959744 | bytes 7340096 | tf_op jit(solution)/shard_map/while/body/eval_jaxpr/kij,kif->kjf/dot_general | solution.py:63
  111.2 6.4 %scatter_fusion.1 = f32[128,256,1]{1,0,2:T(8,128)S(1)} fusion(f32[128,256,1]{1,0,2:T(8,128)S(1)} %select_bitcast_fusion.2, s32[32]{0:T(128)S(1)} %fusion.54, f32[32,128,256]{2,1,0:T(8,128)} %fusion.57), kind=kCustom, calls=%fused_computation.6.clone.clone.1 | custom fusion | flops 1048576 | bytes 12583040 | tf_op jit(solution)/shard_map/while/body/eval_jaxpr/scatter-add | solution.py:66
  117.7 1.8 collective-permute-start
  119.5 1.9 collective-permute-done
  121.6 1.7 gather_fusion.2
  124.0 4.3 %fusion.57 = f32[32,128,256]{2,1,0:T(8,128)} fusion(bf16[32,128,256]{2,1,0:T(8,128)(2,1)S(1)} %gather_fusion.1, bf16[32,128,128]{2,1,0:T(8,128)(2,1)} %gather_fusion.2, bf16[32]{0:T(256)(128)(2,1)S(1)} %fusion.56), kind=kOutput, calls=%fused_computation.17.clone.1 | convolution fusion | flops 268959744 | bytes 7340096 | tf_op jit(solution)/shard_map/while/body/eval_jaxpr/kij,kif->kjf/dot_general | solution.py:63
  128.3 6.4 %scatter_fusion.1 = f32[128,256,1]{1,0,2:T(8,128)S(1)} fusion(f32[128,256,1]{1,0,2:T(8,128)S(1)} %select_bitcast_fusion.2, s32[32]{0:T(128)S(1)} %fusion.54, f32[32,128,256]{2,1,0:T(8,128)} %fusion.57), kind=kCustom, calls=%fused_computation.6.clone.clone.1 | custom fusion | flops 1048576 | bytes 12583040 | tf_op jit(solution)/shard_map/while/body/eval_jaxpr/scatter-add | solution.py:66
  134.8 1.8 collective-permute-start
  136.6 1.9 collective-permute-done
  138.6 6.3 %scatter_fusion.2 = f32[128,256,1]{1,0,2:T(8,128)S(1)} fusion(f32[128,256,1]{1,0,2:T(8,128)S(1)} %bitcast.83, s32[32]{0:T(128)S(1)} %fusion.27, f32[32,128,256]{2,1,0:T(8,128)} %fusion.13), kind=kCustom, calls=%fused_computation.7 | custom fusion | flops 1048576 | bytes 12583040 | tf_op jit(solution)/shard_map/scatter-add | solution.py:66
  144.9 0.7 fusion.16
  145.6 6.0 %all-gather = bf16[512,256]{1,0:T(8,128)(2,1)S(1)} all-gather(bf16[128,256]{1,0:T(8,128)(2,1)S(1)} %get-tuple-element.329), channel_id=2, replica_groups=mesh['row'=4,'col'=8] {'row'}, dimensions={0}, use_global_device_ids=true | all-gather | bytes 327680 | tf_op jit(solution)/shard_map/all_gather | solution.py:75
  151.7 23.5 %while.29 = (s32[]{:T(128)}, f32[8,128,256]{2,1,0:T(8,128)S(1)}, s32[64]{0:T(128)S(1)}, bf16[64,128,128]{2,1,0:T(8,128)(2,1)}, s32[64]{0:T(128)S(1)}, /*index=5*...) while((s32[]{:T(128)}, f32[8,128,256]{2,1,0:T(8,128)S(1)}, ...), condition=%wide.region_8.9_spmd, body=%wide.region_6.8_spmd.sunk | while | flops 135005296 | bytes 12063463 | solution.py:92
  151.9 1.6 gather_fusion
  153.5 1.9 fusion.51
  155.4 2.2 scatter_fusion
  157.7 1.6 gather_fusion
  159.3 1.9 fusion.51
  161.2 2.2 scatter_fusion
  163.6 1.6 gather_fusion
  165.2 1.9 fusion.51
  167.1 2.2 scatter_fusion
  169.5 1.6 gather_fusion
  171.1 1.9 fusion.51
  173.0 2.2 scatter_fusion
  175.2 0.8 convert_element_type.102
  176.0 59.6 %reduce-scatter.2.cloned.1.call-done = bf16[128,256]{1,0:T(8,128)(2,1)} async-done(((bf16[1024,256]{1,0:T(8,128)(2,1)}), bf16[128,256]{1,0:T(8,128)(2,1)}) %reduce-scatter.2.cloned.1.call-update) | async-done | bytes 65552 | tf_op jit(solution)/shard_map/reduce_scatter | solution.py:101
  235.6 1.6 multiply_convert_fusion.1
  (74 shorter events, 5.1 us)
Async XLA Ops:
  7.2 73.1 %copy-start = (bf16[64,128,128]{2,1,0:T(8,128)(2,1)S(1)}, bf16[64,128,128]{2,1,0:T(8,128)(2,1)}, u32[]{:S(2)}) copy-start(bf16[64,128,128]{2,1,0:T(8,128)(2,1)} %param.10) | copy-start | bytes 6291460
  7.2 41.5 %copy-start.3 = (bf16[128,256]{1,0:T(8,128)(2,1)S(1)}, bf16[128,256]{1,0:T(8,128)(2,1)}, u32[]{:S(2)}) copy-start(bf16[128,256]{1,0:T(8,128)(2,1)} %param.9) | copy-start | bytes 196612
  7.2 228.4 %reduce-scatter.2.cloned.1.call-start = ((), (), s32[]{:S(2)}) async-start(), calls=%async_computation.1 | async-start | bytes 589824 | tf_op jit(solution)/shard_map/reduce_scatter | solution.py:101
  95.9 8.4 %copy-start.1 = (bf16[64,128,128]{2,1,0:T(8,128)(2,1)S(1)}, bf16[64,128,128]{2,1,0:T(8,128)(2,1)}, u32[]{:S(2)}) copy-start(bf16[64,128,128]{2,1,0:T(8,128)(2,1)} %get-tuple-element.478) | copy-start | bytes 6291460 | tf_op jit(solution)/shard_map/while
  102.3 2.0 collective-permute-start
  111.2 10.2 %copy-start.1 = (bf16[64,128,128]{2,1,0:T(8,128)(2,1)S(1)}, bf16[64,128,128]{2,1,0:T(8,128)(2,1)}, u32[]{:S(2)}) copy-start(bf16[64,128,128]{2,1,0:T(8,128)(2,1)} %get-tuple-element.478) | copy-start | bytes 6291460 | tf_op jit(solution)/shard_map/while
  117.7 3.7 %collective-permute-start = (bf16[1,128,256]{2,1,0:T(8,128)(2,1)S(1)}, bf16[1,128,256]{2,1,0:T(8,128)(2,1)S(1)}, u32[]{:S(2)}, u32[]{:S(2)}) collective-permute-start(bf16[1,128,256]{2,1,0:T(8,128)(2,1)S(1)} %convert_bitcast_fusion.2), channel_id=1, source_target_pairs={{0,24},{8,0},{16,8},{24,16},{1,25},{9,1},{17,9},{25,17},{2,26},{10... | collective-permute-start | bytes 196616 | tf_op jit(solution)/shard_map/while/body/eval_jaxpr/ppermute | solution.py:11
  128.3 10.2 %copy-start.1 = (bf16[64,128,128]{2,1,0:T(8,128)(2,1)S(1)}, bf16[64,128,128]{2,1,0:T(8,128)(2,1)}, u32[]{:S(2)}) copy-start(bf16[64,128,128]{2,1,0:T(8,128)(2,1)} %get-tuple-element.478) | copy-start | bytes 6291460 | tf_op jit(solution)/shard_map/while
  134.8 3.7 %collective-permute-start = (bf16[1,128,256]{2,1,0:T(8,128)(2,1)S(1)}, bf16[1,128,256]{2,1,0:T(8,128)(2,1)S(1)}, u32[]{:S(2)}, u32[]{:S(2)}) collective-permute-start(bf16[1,128,256]{2,1,0:T(8,128)(2,1)S(1)} %convert_bitcast_fusion.2), channel_id=1, source_target_pairs={{0,24},{8,0},{16,8},{24,16},{1,25},{9,1},{17,9},{25,17},{2,26},{10... | collective-permute-start | bytes 196616 | tf_op jit(solution)/shard_map/while/body/eval_jaxpr/ppermute | solution.py:11
  138.6 6.4 %copy-start.2 = (bf16[128,256]{1,0:T(8,128)(2,1)S(1)}, bf16[128,256]{1,0:T(8,128)(2,1)}, u32[]{:S(2)}) copy-start(bf16[128,256]{1,0:T(8,128)(2,1)} %param.8) | copy-start | bytes 196612
Sparse Core Ops, SparseCore 0:
  176.1 59.4 reduce-scatter.1
where the time goes:
time: 245 us; the launch traced here: 244 us
  blocking collectives  67.5 us (28%)
  waiting for transfers between devices  65.3 us (27%)
  other arithmetic  43.9 us (18%)
  matrix products  25.9 us (11%)
  local copies, waits for them, and re-layouts  21.7 us (9%)
  between operations  15.4 us (6%)
  starting transfers between devices  3.77 us (2%)
    reduce_scatter x1, waiting for transfers between devices, local(): lax.psum_scatter(partial_value.reshape(dst_blocks * tile_len, feat_width)...  59.6 us
    all_gather x1, blocking collectives, local(): lax.all_gather(scaled_grads, 'col', axis=0, tiled=True)  31.5 us
    unnamed x2, blocking collectives  30 us
    scatter-add x4, other arithmetic, backward_add(): return accum_total.at[src_index].add(products)  25.6 us
    dot_general x4, matrix products, backward_add(): jnp.einsum('kij,kif->kjf', chosen, rows[dst_index], preferred_element_typ...  17.9 us
    scatter-add x4, other arithmetic, tile_batch(): return partial_value.at[dst_index].add(products)  8.78 us
    dot_general x4, matrix products, tile_batch(): jnp.einsum('kij,kjf->kif', chosen, everything[src_index], preferred_eleme...  7.47 us
    gather x4, local copies, waits for them, and re-layouts, pick_tiles(): chosen = tile_weight[jnp.maximum(tile_ids, 0)] * keep_mask[:, None, None]  6.93 us
  transfers between devices with their start and end apart: 4, of which 4 were waited for; matrix products, arithmetic and copies ran while one was open for 0% of the time, Pallas kernels for 0%

commit v1 on v0

--- a/solution.py
+++ b/solution.py
@@ -3,6 +3,27 @@
 import jax.numpy as jnp
 from jax import lax
 from jax.sharding import PartitionSpec as P
+
+
+def gather_around(x, axis, dim):
+    size, position, rows = (lax.axis_size(axis), lax.axis_index(axis), x.shape[dim])
+    forward = [(i, (i + 1) % size) for i in range(size)]
+    behind = [(i, (i - 1) % size) for i in range(size)]
+    filled = jnp.zeros((*x.shape[:dim], size * rows, *x.shape[dim + 1 :]), x.dtype)
+    filled = lax.dynamic_update_slice_in_dim(filled, x, position * rows, axis=dim)
+    from_left = from_right = x
+    half = size // 2
+    for turn in range(1, half + 1):
+        from_left = lax.ppermute(from_left, axis, forward)
+        filled = lax.dynamic_update_slice_in_dim(
+            filled, from_left, (position - turn) % size * rows, axis=dim
+        )
+        if turn < size - half:
+            from_right = lax.ppermute(from_right, axis, behind)
+            filled = lax.dynamic_update_slice_in_dim(
+                filled, from_right, (position + turn) % size * rows, axis=dim
+            )
+    return filled
 
 
 def passed_along(value, axis, steps):
@@ -48,9 +69,7 @@
     scaled = (features.astype(jnp.float32) * src_scale[:, None]).astype(jnp.bfloat16)
     scaled = scaled.reshape(src_blocks, tile_len, feat_width)
     scaled_grads = (grad_out.astype(jnp.float32) * dst_scale[:, None]).astype(jnp.bfloat16)
-    grad_rows = lax.all_gather(scaled_grads, "col", axis=0, tiled=True).reshape(
-        dst_blocks, tile_len, feat_width
-    )
+    grad_rows = gather_around(scaled_grads, "col", 0).reshape(dst_blocks, tile_len, feat_width)
 
     def pick_tiles(list_step):
         tile_ids = tile_list[list_step, 0]

time: 245 us -> 234 us (0.955)
  blocking collectives: 67.5 us -> 35.1 us
  starting transfers between devices: 3.77 us -> 18 us
  waiting for transfers between devices: 65.3 us -> 77.3 us
  other arithmetic: 43.9 us -> 41.1 us
    all_gather x1 -> x0, blocking collectives: 31.5 us -> none  [local(): lax.all_gather(scaled_grads, 'col', axis=0, tiled=True)]
    ppermute x0 -> x7, starting transfers between devices: none -> 14.2 us  [the longest x3 14.2 us: gather_around(): from_right = lax.ppermute(from_right, axis, behind)]
    ppermute x0 -> x7, waiting for transfers between devices: none -> 11.3 us  [the longest x4 11.3 us: gather_around(): from_left = lax.ppermute(from_left, axis, forward)]
  transfers between devices with their start and end apart: 4 -> 11, of which waited for: 4 -> 7; matrix products, arithmetic and copies ran while one was open for 0% -> 1% of each run, Pallas kernels for 0% -> 0%
where the time goes in v1:
time: 234 us
  waiting for transfers between devices  77.3 us (33%)
  other arithmetic  41.1 us (18%)
  blocking collectives  35.1 us (15%)
  matrix products  25.9 us (11%)
  local copies, waits for them, and re-layouts  20 us (9%)
  starting transfers between devices  18 us (8%)
  between operations  15.7 us (7%)
    reduce_scatter x1, waiting for transfers between devices, local(): lax.psum_scatter(partial_value.reshape(dst_blocks * tile_len, feat_width)...  60.3 us
    unnamed x2, blocking collectives  28.8 us
    scatter-add x4, other arithmetic, backward_add(): return accum_total.at[src_index].add(products)  25.6 us
    dot_general x4, matrix products, backward_add(): jnp.einsum('kij,kif->kjf', chosen, rows[dst_index], preferred_element_typ...  17.9 us
    ppermute x3, starting transfers between devices, gather_around(): from_right = lax.ppermute(from_right, axis, behind)  14.2 us
    ppermute x4, waiting for transfers between devices, gather_around(): from_left = lax.ppermute(from_left, axis, forward)  11.3 us
    scatter-add x4, other arithmetic, tile_batch(): return partial_value.at[dst_index].add(products)  8.78 us
    dot_general x4, matrix products, tile_batch(): jnp.einsum('kij,kjf->kif', chosen, everything[src_index], preferred_eleme...  7.47 us
  transfers between devices with their start and end apart: 11, of which 7 were waited for; matrix products, arithmetic and copies ran while one was open for 1% of the time, Pallas kernels for 0%

profile of v1, /device:TPU:0, one launch (start us, length us, event | category | flops | bytes accessed | tf_op | source)
XLA Modules:
  0.0 233.6 jit_solution(13121410334265694236)
XLA Ops:
  7.3 0.9 fusion.34
  8.6 2.3 convert_reduce_fusion
  11.1 23.2 %all-reduce.1 = f32[1024]{0:T(1024)S(1)} all-reduce(f32[1024]{0:T(1024)S(1)} %convolution_bitcast_fusion), channel_id=5, replica_groups=mesh['row'=4,'col'=8] {'col'}, use_global_device_ids=true, to_apply=%region_11.12.clone | all-reduce | flops 1024 | bytes 8192
  35.8 4.7 %collective-permute-start.2 = (bf16[128,256]{1,0:T(8,128)(2,1)S(1)}, bf16[128,256]{1,0:T(8,128)(2,1)S(1)}, u32[]{:S(2)}, u32[]{:S(2)}) collective-permute-start(bf16[128,256]{1,0:T(8,128)(2,1)S(1)} %get-tuple-element.324), channel_id=1, source_target_pairs={{0,7},{1,0},{2,1},{3,2},{4,3},{5,4},{6,5},{7,6},{8,15},{9,8},{10,9... | collective-permute-start | bytes 196616 | tf_op jit(solution)/shard_map/ppermute | solution.py:22
  42.2 5.7 %all-reduce = f32[512]{0:T(512)S(1)} all-reduce(f32[512]{0:T(512)S(1)} %convolution_bitcast_fusion.1), channel_id=3, replica_groups=mesh['row'=4,'col'=8] {'row'}, use_global_device_ids=true, to_apply=%region_5.6.clone | all-reduce | flops 512 | bytes 4096
  47.9 1.7 gather_fusion.3
  49.7 4.7 %collective-permute-start.4 = (bf16[128,256]{1,0:T(8,128)(2,1)S(1)}, bf16[128,256]{1,0:T(8,128)(2,1)S(1)}, u32[]{:S(2)}, u32[]{:S(2)}) collective-permute-start(bf16[128,256]{1,0:T(8,128)(2,1)S(1)} %collective-permute-done.2), channel_id=1, source_target_pairs={{0,7},{1,0},{2,1},{3,2},{4,3},{5,4},{6,5},{7,6},{8,15},{9,8},{10,9... | collective-permute-start | bytes 196616 | tf_op jit(solution)/shard_map/ppermute | solution.py:22
  54.4 2.2 collective-permute-done.3
  56.6 4.7 %collective-permute-start.6 = (bf16[128,256]{1,0:T(8,128)(2,1)S(1)}, bf16[128,256]{1,0:T(8,128)(2,1)S(1)}, u32[]{:S(2)}, u32[]{:S(2)}) collective-permute-start(bf16[128,256]{1,0:T(8,128)(2,1)S(1)} %collective-permute-done.4), channel_id=1, source_target_pairs={{0,7},{1,0},{2,1},{3,2},{4,3},{5,4},{6,5},{7,6},{8,15},{9,8},{10,9... | collective-permute-start | bytes 196616 | tf_op jit(solution)/shard_map/ppermute | solution.py:22
  61.4 2.2 collective-permute-done.5
  63.6 6.9 %collective-permute-done.7 = bf16[128,256]{1,0:T(8,128)(2,1)S(1)} collective-permute-done((bf16[128,256]{1,0:T(8,128)(2,1)S(1)}, bf16[128,256]{1,0:T(8,128)(2,1)S(1)}, u32[]{:S(2)}, u32[]{:S(2)}) %collective-permute-start.7) | collective-permute-done | bytes 65568 | tf_op jit(solution)/shard_map/ppermute | solution.py:17
  70.6 2.0 gather_fusion.4
  72.6 5.0 %fusion.13 = f32[32,128,256]{2,1,0:T(8,128)} fusion(bf16[32,128,256]{2,1,0:T(8,128)(2,1)} %gather_fusion.4, bf16[32,128,128]{2,1,0:T(8,128)(2,1)} %gather_fusion.3, bf16[32]{0:T(256)(128)(2,1)S(1)} %fusion.26), kind=kOutput, calls=%fused_computation.41 | convolution fusion | flops 268959744 | bytes 7340096 | tf_op jit(solution)/shard_map/kij,kif->kjf/dot_general | solution.py:82
  77.6 49.5 %while.30 = (s32[]{:T(128)}, f32[1,128,256]{2,1,0:T(8,128)S(1)}, s32[4,3,32]{2,1,0:T(4,128)S(1)}, bf16[64,128,128]{2,1,0:T(8,128)(2,1)S(1)}, bf16[8,128,256]{2,1...) while((s32[]{:T(128)}, f32[1,128,256]{2,1,0:T(8,128)S(1)}, ...), condition=%wide.region_14.15_spmd.clone, body=%wide.region_12.14_spmd.clone.sunk | while | flops 270109056 | bytes 35530608 | solution.py:116
  77.7 1.7 gather_fusion.2
  79.4 0.7 gather_fusion.1
  80.1 4.3 %fusion.57 = f32[32,128,256]{2,1,0:T(8,128)} fusion(bf16[32,128,256]{2,1,0:T(8,128)(2,1)S(1)} %gather_fusion.1, bf16[32,128,128]{2,1,0:T(8,128)(2,1)} %gather_fusion.2, bf16[32]{0:T(256)(128)(2,1)S(1)} %fusion.56), kind=kOutput, calls=%fused_computation.17.clone.1 | convolution fusion | flops 268959744 | bytes 7340096 | tf_op jit(solution)/shard_map/while/body/eval_jaxpr/kij,kif->kjf/dot_general | solution.py:82
  84.4 6.4 %scatter_fusion.1 = f32[128,256,1]{1,0,2:T(8,128)S(1)} fusion(f32[128,256,1]{1,0,2:T(8,128)S(1)} %select_bitcast_fusion.2, s32[32]{0:T(128)S(1)} %fusion.54, f32[32,128,256]{2,1,0:T(8,128)} %fusion.57), kind=kCustom, calls=%fused_computation.6.clone.clone.1 | custom fusion | flops 1048576 | bytes 12583040 | tf_op jit(solution)/shard_map/while/body/eval_jaxpr/scatter-add | solution.py:85
  90.9 1.9 collective-permute-done
  93.0 1.7 gather_fusion.2
  95.4 4.3 %fusion.57 = f32[32,128,256]{2,1,0:T(8,128)} fusion(bf16[32,128,256]{2,1,0:T(8,128)(2,1)S(1)} %gather_fusion.1, bf16[32,128,128]{2,1,0:T(8,128)(2,1)} %gather_fusion.2, bf16[32]{0:T(256)(128)(2,1)S(1)} %fusion.56), kind=kOutput, calls=%fused_computation.17.clone.1 | convolution fusion | flops 268959744 | bytes 7340096 | tf_op jit(solution)/shard_map/while/body/eval_jaxpr/kij,kif->kjf/dot_general | solution.py:82
  99.7 6.4 %scatter_fusion.1 = f32[128,256,1]{1,0,2:T(8,128)S(1)} fusion(f32[128,256,1]{1,0,2:T(8,128)S(1)} %select_bitcast_fusion.2, s32[32]{0:T(128)S(1)} %fusion.54, f32[32,128,256]{2,1,0:T(8,128)} %fusion.57), kind=kCustom, calls=%fused_computation.6.clone.clone.1 | custom fusion | flops 1048576 | bytes 12583040 | tf_op jit(solution)/shard_map/while/body/eval_jaxpr/scatter-add | solution.py:85
  106.2 1.8 collective-permute-start
  108.0 1.9 collective-permute-done
  110.1 1.7 gather_fusion.2
  112.5 4.3 %fusion.57 = f32[32,128,256]{2,1,0:T(8,128)} fusion(bf16[32,128,256]{2,1,0:T(8,128)(2,1)S(1)} %gather_fusion.1, bf16[32,128,128]{2,1,0:T(8,128)(2,1)} %gather_fusion.2, bf16[32]{0:T(256)(128)(2,1)S(1)} %fusion.56), kind=kOutput, calls=%fused_computation.17.clone.1 | convolution fusion | flops 268959744 | bytes 7340096 | tf_op jit(solution)/shard_map/while/body/eval_jaxpr/kij,kif->kjf/dot_general | solution.py:82
  116.8 6.4 %scatter_fusion.1 = f32[128,256,1]{1,0,2:T(8,128)S(1)} fusion(f32[128,256,1]{1,0,2:T(8,128)S(1)} %select_bitcast_fusion.2, s32[32]{0:T(128)S(1)} %fusion.54, f32[32,128,256]{2,1,0:T(8,128)} %fusion.57), kind=kCustom, calls=%fused_computation.6.clone.clone.1 | custom fusion | flops 1048576 | bytes 12583040 | tf_op jit(solution)/shard_map/while/body/eval_jaxpr/scatter-add | solution.py:85
  123.3 1.8 collective-permute-start
  125.1 1.9 collective-permute-done
  127.1 6.3 %scatter_fusion.2 = f32[128,256,1]{1,0,2:T(8,128)S(1)} fusion(f32[128,256,1]{1,0,2:T(8,128)S(1)} %bitcast.83, s32[32]{0:T(128)S(1)} %fusion.27, f32[32,128,256]{2,1,0:T(8,128)} %fusion.13), kind=kCustom, calls=%fused_computation.7 | custom fusion | flops 1048576 | bytes 12583040 | tf_op jit(solution)/shard_map/scatter-add | solution.py:85
  133.4 0.7 fusion.16
  134.1 6.3 %all-gather = bf16[512,256]{1,0:T(8,128)(2,1)S(1)} all-gather(bf16[128,256]{1,0:T(8,128)(2,1)S(1)} %get-tuple-element.331), channel_id=2, replica_groups=mesh['row'=4,'col'=8] {'row'}, dimensions={0}, use_global_device_ids=true | all-gather | bytes 327680 | tf_op jit(solution)/shard_map/all_gather | solution.py:94
  140.6 23.5 %while.29 = (s32[]{:T(128)}, f32[8,128,256]{2,1,0:T(8,128)S(1)}, s32[64]{0:T(128)S(1)}, bf16[64,128,128]{2,1,0:T(8,128)(2,1)}, s32[64]{0:T(128)S(1)}, /*index=5*...) while((s32[]{:T(128)}, f32[8,128,256]{2,1,0:T(8,128)S(1)}, ...), condition=%wide.region_8.9_spmd, body=%wide.region_6.8_spmd.sunk | while | flops 135005296 | bytes 12063463 | solution.py:111
  140.7 1.6 gather_fusion
  142.3 1.9 fusion.51
  144.2 2.2 scatter_fusion
  146.6 1.6 gather_fusion
  148.2 1.9 fusion.51
  150.1 2.2 scatter_fusion
  152.5 1.6 gather_fusion
  154.1 1.9 fusion.51
  156.0 2.2 scatter_fusion
  158.4 1.6 gather_fusion
  160.0 1.9 fusion.51
  161.8 2.2 scatter_fusion
  164.0 0.8 convert_element_type.102
  164.9 60.3 %reduce-scatter.2.cloned.1.call-done = bf16[128,256]{1,0:T(8,128)(2,1)} async-done(((bf16[1024,256]{1,0:T(8,128)(2,1)}), bf16[128,256]{1,0:T(8,128)(2,1)}) %reduce-scatter.2.cloned.1.call-update) | async-done | bytes 65552 | tf_op jit(solution)/shard_map/reduce_scatter | solution.py:120
  225.2 1.6 multiply_convert_fusion.1
  (101 shorter events, 5.2 us)
Async XLA Ops:
  7.2 27.1 %copy-start.6 = (u32[32]{0:T(128)S(1)}, u32[32]{0:T(128)}, u32[]{:S(2)}) copy-start(u32[32]{0:T(128)} %constant.228) | copy-start | bytes 388
  7.2 33.4 %copy-start.5 = (u32[32]{0:T(128)S(1)}, u32[32]{0:T(128)}, u32[]{:S(2)}) copy-start(u32[32]{0:T(128)} %constant.224) | copy-start | bytes 388
  7.2 33.3 %copy-start.4 = (s32[4,3,32]{2,0,1:T(4,128)S(1)}, s32[4,3,32]{2,0,1:T(4,128)}, u32[]{:S(2)}) copy-start(s32[4,3,32]{2,0,1:T(4,128)} %param.11) | copy-start | bytes 4612
  7.2 40.7 %copy-start = (bf16[64,128,128]{2,1,0:T(8,128)(2,1)S(1)}, bf16[64,128,128]{2,1,0:T(8,128)(2,1)}, u32[]{:S(2)}) copy-start(bf16[64,128,128]{2,1,0:T(8,128)(2,1)} %param.10) | copy-start | bytes 6291460
  7.2 28.4 %copy-start.2 = (bf16[128,256]{1,0:T(8,128)(2,1)S(1)}, bf16[128,256]{1,0:T(8,128)(2,1)}, u32[]{:S(2)}) copy-start(bf16[128,256]{1,0:T(8,128)(2,1)} %param.9) | copy-start | bytes 196612
  7.2 218.0 %reduce-scatter.2.cloned.1.call-start = ((), (), s32[]{:S(2)}) async-start(), calls=%async_computation.1 | async-start | bytes 589824 | tf_op jit(solution)/shard_map/reduce_scatter | solution.py:120
  35.7 13.9 %collective-permute-start.1 = (bf16[128,256]{1,0:T(8,128)(2,1)S(1)}, bf16[128,256]{1,0:T(8,128)(2,1)S(1)}, u32[]{:S(2)}, u32[]{:S(2)}) collective-permute-start(bf16[128,256]{1,0:T(8,128)(2,1)S(1)} %get-tuple-element.324), channel_id=1, source_target_pairs={{0,1},{1,2},{2,3},{3,4},{4,5},{5,6},{6,7},{7,0},{8,9},{9,10},{10,1... | collective-permute-start | bytes 196616 | tf_op jit(solution)/shard_map/ppermute | solution.py:17
  35.8 13.9 %collective-permute-start.2 = (bf16[128,256]{1,0:T(8,128)(2,1)S(1)}, bf16[128,256]{1,0:T(8,128)(2,1)S(1)}, u32[]{:S(2)}, u32[]{:S(2)}) collective-permute-start(bf16[128,256]{1,0:T(8,128)(2,1)S(1)} %get-tuple-element.324), channel_id=1, source_target_pairs={{0,7},{1,0},{2,1},{3,2},{4,3},{5,4},{6,5},{7,6},{8,15},{9,8},{10,9... | collective-permute-start | bytes 196616 | tf_op jit(solution)/shard_map/ppermute | solution.py:22
  49.7 7.0 %collective-permute-start.3 = (bf16[128,256]{1,0:T(8,128)(2,1)S(1)}, bf16[128,256]{1,0:T(8,128)(2,1)S(1)}, u32[]{:S(2)}, u32[]{:S(2)}) collective-permute-start(bf16[128,256]{1,0:T(8,128)(2,1)S(1)} %collective-permute-done.1), channel_id=1, source_target_pairs={{0,1},{1,2},{2,3},{3,4},{4,5},{5,6},{6,7},{7,0},{8,9},{9,10},{10,1... | collective-permute-start | bytes 196616 | tf_op jit(solution)/shard_map/ppermute | solution.py:17
  49.7 7.0 %collective-permute-start.4 = (bf16[128,256]{1,0:T(8,128)(2,1)S(1)}, bf16[128,256]{1,0:T(8,128)(2,1)S(1)}, u32[]{:S(2)}, u32[]{:S(2)}) collective-permute-start(bf16[128,256]{1,0:T(8,128)(2,1)S(1)} %collective-permute-done.2), channel_id=1, source_target_pairs={{0,7},{1,0},{2,1},{3,2},{4,3},{5,4},{6,5},{7,6},{8,15},{9,8},{10,9... | collective-permute-start | bytes 196616 | tf_op jit(solution)/shard_map/ppermute | solution.py:22
  56.6 7.0 %collective-permute-start.5 = (bf16[128,256]{1,0:T(8,128)(2,1)S(1)}, bf16[128,256]{1,0:T(8,128)(2,1)S(1)}, u32[]{:S(2)}, u32[]{:S(2)}) collective-permute-start(bf16[128,256]{1,0:T(8,128)(2,1)S(1)} %collective-permute-done.3), channel_id=1, source_target_pairs={{0,1},{1,2},{2,3},{3,4},{4,5},{5,6},{6,7},{7,0},{8,9},{9,10},{10,1... | collective-permute-start | bytes 196616 | tf_op jit(solution)/shard_map/ppermute | solution.py:17
  56.6 7.0 %collective-permute-start.6 = (bf16[128,256]{1,0:T(8,128)(2,1)S(1)}, bf16[128,256]{1,0:T(8,128)(2,1)S(1)}, u32[]{:S(2)}, u32[]{:S(2)}) collective-permute-start(bf16[128,256]{1,0:T(8,128)(2,1)S(1)} %collective-permute-done.4), channel_id=1, source_target_pairs={{0,7},{1,0},{2,1},{3,2},{4,3},{5,4},{6,5},{7,6},{8,15},{9,8},{10,9... | collective-permute-start | bytes 196616 | tf_op jit(solution)/shard_map/ppermute | solution.py:22
  63.6 7.0 %collective-permute-start.7 = (bf16[128,256]{1,0:T(8,128)(2,1)S(1)}, bf16[128,256]{1,0:T(8,128)(2,1)S(1)}, u32[]{:S(2)}, u32[]{:S(2)}) collective-permute-start(bf16[128,256]{1,0:T(8,128)(2,1)S(1)} %collective-permute-done.5), channel_id=1, source_target_pairs={{0,1},{1,2},{2,3},{3,4},{4,5},{5,6},{6,7},{7,0},{8,9},{9,10},{10,1... | collective-permute-start | bytes 196616 | tf_op jit(solution)/shard_map/ppermute | solution.py:17
  84.4 8.4 %copy-start.1 = (bf16[64,128,128]{2,1,0:T(8,128)(2,1)S(1)}, bf16[64,128,128]{2,1,0:T(8,128)(2,1)}, u32[]{:S(2)}) copy-start(bf16[64,128,128]{2,1,0:T(8,128)(2,1)} %get-tuple-element.480) | copy-start | bytes 6291460 | tf_op jit(solution)/shard_map/while
  90.8 2.0 collective-permute-start
  99.7 10.2 %copy-start.1 = (bf16[64,128,128]{2,1,0:T(8,128)(2,1)S(1)}, bf16[64,128,128]{2,1,0:T(8,128)(2,1)}, u32[]{:S(2)}) copy-start(bf16[64,128,128]{2,1,0:T(8,128)(2,1)} %get-tuple-element.480) | copy-start | bytes 6291460 | tf_op jit(solution)/shard_map/while
  106.2 3.7 %collective-permute-start = (bf16[1,128,256]{2,1,0:T(8,128)(2,1)S(1)}, bf16[1,128,256]{2,1,0:T(8,128)(2,1)S(1)}, u32[]{:S(2)}, u32[]{:S(2)}) collective-permute-start(bf16[1,128,256]{2,1,0:T(8,128)(2,1)S(1)} %convert_bitcast_fusion.2), channel_id=1, source_target_pairs={{0,24},{8,0},{16,8},{24,16},{1,25},{9,1},{17,9},{25,17},{2,26},{10... | collective-permute-start | bytes 196616 | tf_op jit(solution)/shard_map/while/body/eval_jaxpr/ppermute | solution.py:32
  116.8 10.2 %copy-start.1 = (bf16[64,128,128]{2,1,0:T(8,128)(2,1)S(1)}, bf16[64,128,128]{2,1,0:T(8,128)(2,1)}, u32[]{:S(2)}) copy-start(bf16[64,128,128]{2,1,0:T(8,128)(2,1)} %get-tuple-element.480) | copy-start | bytes 6291460 | tf_op jit(solution)/shard_map/while
  123.3 3.7 %collective-permute-start = (bf16[1,128,256]{2,1,0:T(8,128)(2,1)S(1)}, bf16[1,128,256]{2,1,0:T(8,128)(2,1)S(1)}, u32[]{:S(2)}, u32[]{:S(2)}) collective-permute-start(bf16[1,128,256]{2,1,0:T(8,128)(2,1)S(1)} %convert_bitcast_fusion.2), channel_id=1, source_target_pairs={{0,24},{8,0},{16,8},{24,16},{1,25},{9,1},{17,9},{25,17},{2,26},{10... | collective-permute-start | bytes 196616 | tf_op jit(solution)/shard_map/while/body/eval_jaxpr/ppermute | solution.py:32
  127.1 6.4 %copy-start.3 = (bf16[128,256]{1,0:T(8,128)(2,1)S(1)}, bf16[128,256]{1,0:T(8,128)(2,1)}, u32[]{:S(2)}) copy-start(bf16[128,256]{1,0:T(8,128)(2,1)} %param.8) | copy-start | bytes 196612
Sparse Core Ops, SparseCore 0:
  165.0 60.1 reduce-scatter.1
